TPU v7x, 32 devices: a whole 2x2x4 slice. The times are simulated.
32 devices in a mesh: row: 4 (over z), col: 8 (over y, x, core).
Axes of the slice: x: 2, y: 2, z: 4, core: 2. Of those that a mesh axis runs over, the one named last changes fastest.
Arguments:
- resistance: float32 [768, 1024], P('row', 'col'), may hold values from 1 to 100
- ground: float32 [768, 1024], P('row', 'col'), may hold values from 0.001 to 0.01
- nodata: int32 [768, 1024], P('row', 'col'), may hold values 0 or 1
- patch_ids: int32 [768, 1024], P('row', 'col'), may hold values from 0 to 8
Outputs:
- correction: float32 [8, 768, 1024], P(None, 'row', 'col')
All inputs are finite; a program needn't handle non-finite values. No bound on the sum of `nodata` on one device may be relied on, other than what follows from the above.
Results may differ from a plain program's by a relative error of at most 0.0003.
Values sent between devices are 32-bit elements; how exact they have to be, the bound alone decides.
No kernel may reach another device: no remote copies, remote signals or barrier semaphores. Data moves between devices by JAX's collectives and lax.ppermute only.
A program may use at most 128 MiB of HBM per device.

v0:
```python
from functools import partial
import jax
import jax.numpy as jnp
from jax import lax
from jax.sharding import PartitionSpec as P

RHS = 8
ITERS = 4
OMEGA = 0.8


def padded_2(block, sides, width):
    for axis, dim in sides:
        count = lax.axis_size(axis)
        forward = [(i, i + 1) for i in range(count - 1)]
        backward = [(target, source) for source, target in forward]
        low = lax.ppermute(
            lax.slice_in_dim(block, block.shape[dim] - width, None, axis=dim), axis, forward
        )
        high = lax.ppermute(lax.slice_in_dim(block, 0, width, axis=dim), axis, backward)
        block = jnp.concatenate([low, block, high], axis=dim)
    return block


def shifted(block, axis, distance):
    devices = range(lax.axis_size(axis))
    route = [(i - distance, i) for i in devices if i - distance in devices]
    return lax.ppermute(block, axis, route)


def partner_2(shard, axis, apart):
    return lax.ppermute(shard, axis, [(i, i ^ 1 << apart) for i in range(lax.axis_size(axis))])


def conductance(resist, validity, near_resist, near_valid):
    return validity * near_valid * (2.0 / (resist + near_resist))


def edge_terms(res_pad, val_pad):
    resist = res_pad[1:-1, 1:-1]
    validity = val_pad[1:-1, 1:-1]
    north_link = conductance(resist, validity, res_pad[:-2, 1:-1], val_pad[:-2, 1:-1])
    south_link = conductance(resist, validity, res_pad[2:, 1:-1], val_pad[2:, 1:-1])
    west_link = conductance(resist, validity, res_pad[1:-1, :-2], val_pad[1:-1, :-2])
    east_link = conductance(resist, validity, res_pad[1:-1, 2:], val_pad[1:-1, 2:])
    return (north_link, south_link, west_link, east_link)


def diagonal_of(coeffs):
    return coeffs[0] + coeffs[1] + coeffs[2] + coeffs[3] + coeffs[4]


def apply_operator(values, coeffs, sides):
    above_cells, below_cells, left_cells, right_cells = sides
    pulled = (
        coeffs[1] * above_cells
        + coeffs[2] * below_cells
        + coeffs[3] * left_cells
        + coeffs[4] * right_cells
    )
    return diagonal_of(coeffs) * values - pulled


def restrict_field(values):
    count, rows_here, cols_here = values.shape
    return values.reshape(count, rows_here // 2, 2, cols_here // 2, 2).sum(axis=(2, 4))


def coarse_coeffs(coeffs):
    count, rows_here, cols_here = coeffs.shape
    blocks = coeffs.reshape(count, rows_here // 2, 2, cols_here // 2, 2)
    leakage = blocks[0].sum(axis=(1, 3))
    north_link = blocks[1][:, 0].sum(axis=-1)
    south_link = blocks[2][:, 1].sum(axis=-1)
    west_link = blocks[3][:, :, :, 0].sum(axis=1)
    east_link = blocks[4][:, :, :, 1].sum(axis=1)
    return jnp.stack([leakage, north_link, south_link, west_link, east_link])


def prolong(values):
    return jnp.repeat(jnp.repeat(values, 2, axis=1), 2, axis=2)


def halo_sides(values):
    padded = padded_2(values, (("row", 1), ("col", 2)), 1)
    return (padded[:, :-2, 1:-1], padded[:, 2:, 1:-1], padded[:, 1:-1, :-2], padded[:, 1:-1, 2:])


def rim_sides(values, distance):
    above_rim = shifted(values[:, -1:, :], "row", distance)
    below_rim = shifted(values[:, :1, :], "row", -distance)
    left_rim = shifted(values[:, :, -1:], "col", distance)
    right_rim = shifted(values[:, :, :1], "col", -distance)
    above_cells = jnp.concatenate([above_rim, values[:, :-1, :]], axis=1)
    below_cells = jnp.concatenate([values[:, 1:, :], below_rim], axis=1)
    left_cells = jnp.concatenate([left_rim, values[:, :, :-1]], axis=2)
    right_cells = jnp.concatenate([values[:, :, 1:], right_rim], axis=2)
    return (above_cells, below_cells, left_cells, right_cells)


def descend(residual, coeffs, sides_of):
    smoothed = OMEGA * residual / diagonal_of(coeffs)
    remainder = residual - apply_operator(smoothed, coeffs, sides_of(smoothed))
    return (smoothed, restrict_field(remainder), coarse_coeffs(coeffs))


def merge_tiles(payload, bit_index):
    partner = partner_2(payload, "row", bit_index)
    is_first = (lax.axis_index("row") >> bit_index) % 2 == 0
    payload = jnp.where(
        is_first,
        jnp.concatenate([payload, partner], axis=1),
        jnp.concatenate([partner, payload], axis=1),
    )
    partner = partner_2(payload, "col", bit_index)
    is_first = (lax.axis_index("col") >> bit_index) % 2 == 0
    return jnp.where(
        is_first,
        jnp.concatenate([payload, partner], axis=2),
        jnp.concatenate([partner, payload], axis=2),
    )


def merge_level(residual, coeffs, bit_index):
    sources = residual.shape[0]
    merged = merge_tiles(jnp.concatenate([residual, coeffs], axis=0), bit_index)
    return (merged[:sources], merged[sources:])


def own_part(whole_grid, shift_bits, pieces, rows_here, cols_here):
    row_at = (lax.axis_index("row") >> shift_bits) % pieces
    col_at = (lax.axis_index("col") >> shift_bits) % pieces
    starts = (jnp.int32(0), row_at * rows_here, col_at * cols_here)
    return lax.dynamic_slice(whole_grid, starts, (whole_grid.shape[0], rows_here, cols_here))


def coarse_solve(rhs_grid, coeffs):
    sides_of = partial(rim_sides, distance=4)
    owner_weight = jnp.logical_and(
        lax.axis_index("row") % 4 == 0, lax.axis_index("col") % 4 == 0
    ).astype(jnp.float32)

    def local_dot(first, second):
        return owner_weight * jnp.sum(first * second, axis=(1, 2))

    def norm_sum(values):
        return lax.psum(local_dot(values, values), ("row", "col"))

    def expand(scalars):
        return scalars[:, None, None]

    solution = jnp.zeros_like(rhs_grid)
    residual = rhs_grid
    direction = residual
    norm_now = norm_sum(residual)
    for sweep in range(ITERS):
        image = apply_operator(direction, coeffs, sides_of(direction))
        step_size = norm_now / lax.psum(local_dot(direction, image), ("row", "col"))
        solution = solution + expand(step_size) * direction
        if sweep + 1 < ITERS:
            residual = residual - expand(step_size) * image
            norm_next = norm_sum(residual)
            direction = residual + expand(norm_next / norm_now) * direction
            norm_now = norm_next
    return solution


def shards(resistance, ground, nodata, patch_ids):
    validity = (nodata == 0).astype(jnp.float32)
    padded = padded_2(jnp.stack([resistance, validity]), (("row", 1), ("col", 2)), 1)
    coeffs = jnp.stack([ground] + list(edge_terms(padded[0], padded[1])))
    sources = jnp.arange(RHS, dtype=jnp.int32)[:, None, None]
    residual = validity[None] * (
        (patch_ids[None] == sources + 1).astype(jnp.float32)
        - 0.125 * (patch_ids[None] > 0).astype(jnp.float32)
    )
    smooth_a, residual, coeffs_b = descend(residual, coeffs, halo_sides)
    smooth_b, residual, coeffs_c = descend(residual, coeffs_b, halo_sides)
    smooth_c, residual, coeffs_d = descend(residual, coeffs_c, halo_sides)
    rows_d = residual.shape[1]
    cols_d = residual.shape[2]
    residual, coeffs_d = merge_level(residual, coeffs_d, 0)
    smooth_d, residual, coeffs_e = descend(residual, coeffs_d, partial(rim_sides, distance=2))
    residual, coeffs_e = merge_level(residual, coeffs_e, 1)
    solution = coarse_solve(residual, coeffs_e)
    upward = smooth_d + own_part(prolong(solution), 1, 2, 2 * rows_d, 2 * cols_d)
    upward = own_part(prolong(upward), 0, 2, 2 * rows_d, 2 * cols_d)
    upward = smooth_c + upward
    upward = smooth_b + prolong(upward)
    return smooth_a + prolong(upward)


def solution(mesh):
    in_specs = (P("row", "col"), P("row", "col"), P("row", "col"), P("row", "col"))
    out_specs = P(None, "row", "col")
    return jax.shard_map(shards, mesh=mesh, in_specs=in_specs, out_specs=out_specs, check_vma=False)
```

profile of v0, /device:TPU:0, one launch (start us, length us, event | category | flops | bytes accessed | tf_op | source)
XLA Modules:
  0.0 562.9 jit_solution(4791267187569328202)
XLA Ops:
  1.6 4.9 collective-permute-start
  17.3 8.4 %squeeze.46 = f32[96,2,64,2]{3,2,1,0:T(8,128)} reshape(f32[192,128]{1,0:T(8,128)} %param.5) | data formatting | bytes 196608 | tf_op jit(solution)/shard_map/squeeze | solution.py:72
  34.1 7.6 %squeeze.47 = f32[96,2,64,2]{3,2,1,0:T(8,128)} reshape(f32[192,128]{1,0:T(8,128)S(1)} %get-tuple-element.19) | data formatting | bytes 196608 | tf_op jit(solution)/shard_map/squeeze | solution.py:73
  41.6 7.6 %squeeze.48 = f32[96,2,64,2]{3,2,1,0:T(8,128)} reshape(f32[192,128]{1,0:T(8,128)S(1)} %get-tuple-element.20) | data formatting | bytes 196608 | tf_op jit(solution)/shard_map/squeeze | solution.py:74
  49.2 4.6 slice_reduce_fusion.2
  54.0 7.6 %squeeze.49 = f32[96,2,64,2]{3,2,1,0:T(8,128)} reshape(f32[192,128]{1,0:T(8,128)S(1)} %get-tuple-element.21) | data formatting | bytes 196608 | tf_op jit(solution)/shard_map/squeeze | solution.py:75
  61.6 7.8 %squeeze.50 = f32[96,2,64,2]{3,2,1,0:T(8,128)} reshape(f32[192,128]{1,0:T(8,128)S(1)} %get-tuple-element.22) | data formatting | bytes 196608 | tf_op jit(solution)/shard_map/squeeze | solution.py:76
  69.4 7.9 %slice_reduce_fusion = (f32[96,64]{1,0:T(8,128)S(1)}, f32[96,64]{1,0:T(8,128)S(1)}) fusion(f32[96,2,64,2]{3,2,1,0:T(8,128)} %squeeze.50, f32[96,2,64,2]{3,2,1,0:T(8,128)} %squeeze.49), kind=kLoop, calls=%fused_computation | loop fusion | flops 12288 | bytes 147456 | tf_op jit(solution)/shard_map/reduce_sum | solution.py:76
  91.8 8.8 %collective-permute-done.4 = f32[8,1,128]{1,0,2:T(8,128)S(1)} collective-permute-done((f32[8,1,128]{1,0,2:T(8,128)S(1)}, f32[8,1,128]{1,0,2:T(8,128)S(1)}, u32[]{:S(2)}, u32[]{:S(2)}) %collective-permute-start.4) | collective-permute-done | bytes 4128 | tf_op jit(solution)/shard_map/ppermute | solution.py:17
  100.6 4.7 collective-permute-done.5
  115.4 4.1 fusion.3
  119.5 7.0 %copy.453 = f32[8,192,128]{0,2,1:T(8,128)} copy(f32[8,192,128]{1,0,2:T(8,128)S(1)} %fusion.3) | data formatting | bytes 1572864 | tf_op jit(solution)/shard_map/sub | solution.py:103
  126.5 14.0 %reduce_sum.288 = f32[8,96,64]{0,2,1:T(8,128)S(1)} reduce(f32[8,96,2,64,2]{0,4,3,2,1:T(2,128)} %bitcast.80, f32[]{:T(128)} %constant.67.clone.1), dimensions={2,4}, to_apply=%region_0.0 | reduce | flops 147456 | bytes 983044 | tf_op jit(solution)/shard_map/reduce_sum | solution.py:66
  150.9 4.7 collective-permute-done.9
  155.7 4.1 collective-permute-start.10
  198.2 5.9 %collective-permute-done.16 = f32[13,24,16]{0,2,1:T(8,128)S(1)} collective-permute-done((f32[13,24,16]{0,2,1:T(8,128)S(1)}, f32[13,24,16]{0,2,1:T(8,128)S(1)}, u32[]{:S(2)}, u32[]{:S(2)}) %collective-permute-start.16) | collective-permute-done | bytes 20000 | tf_op jit(solution)/shard_map/ppermute | solution.py:32
  209.7 4.5 collective-permute-start.20
  225.4 7.4 %collective-permute-done.22 = f32[13,24,16]{0,2,1:T(8,128)S(1)} collective-permute-done((f32[13,24,16]{0,2,1:T(8,128)S(1)}, f32[13,24,16]{0,2,1:T(8,128)S(1)}, u32[]{:S(2)}, u32[]{:S(2)}) %collective-permute-start.22) | collective-permute-done | bytes 20000 | tf_op jit(solution)/shard_map/ppermute | solution.py:32
  244.9 4.2 collective-permute-done.27
  249.3 37.8 %all-reduce = (f32[8]{0:T(128)S(1)}, f32[8]{0:T(128)S(1)}) all-reduce(f32[8]{0:T(128)S(1)} %broadcast_multiply_fusion.7, f32[8]{0:T(128)S(1)} %broadcast_multiply_fusion.6), channel_id=1, replica_groups=mesh['row'=4,'col'=8] {'row','col'}, use_global_device_ids=true, to_apply=%region_25.26 | all-reduce | flops 16 | bytes 128 | tf_op jit(solution)/shard_map/psum | solution.py:147
  287.3 40.3 %psum.58 = f32[8]{0:T(128)S(1)} all-reduce(f32[8]{0:T(128)S(1)} %broadcast_multiply_fusion.5), channel_id=1, replica_groups=mesh['row'=4,'col'=8] {'row','col'}, use_global_device_ids=true, to_apply=%region_29.30 | all-reduce | flops 8 | bytes 64 | tf_op jit(solution)/shard_map/psum | solution.py:147
  329.2 4.2 collective-permute-start.30
  334.7 4.1 collective-permute-done.31
  339.1 37.6 %psum.59 = f32[8]{0:T(128)S(1)} all-reduce(f32[8]{0:T(128)S(1)} %broadcast_multiply_fusion.4), channel_id=1, replica_groups=mesh['row'=4,'col'=8] {'row','col'}, use_global_device_ids=true, to_apply=%region_31.32 | all-reduce | flops 8 | bytes 64 | tf_op jit(solution)/shard_map/psum | solution.py:158
  377.0 41.9 %psum.60 = f32[8]{0:T(128)S(1)} all-reduce(f32[8]{0:T(128)S(1)} %broadcast_multiply_fusion.3), channel_id=1, replica_groups=mesh['row'=4,'col'=8] {'row','col'}, use_global_device_ids=true, to_apply=%region_33.34 | all-reduce | flops 8 | bytes 64 | tf_op jit(solution)/shard_map/psum | solution.py:147
  420.5 4.2 collective-permute-start.34
  426.1 4.1 collective-permute-done.35
  430.5 37.6 %psum.61 = f32[8]{0:T(128)S(1)} all-reduce(f32[8]{0:T(128)S(1)} %broadcast_multiply_fusion.2), channel_id=1, replica_groups=mesh['row'=4,'col'=8] {'row','col'}, use_global_device_ids=true, to_apply=%region_35.36 | all-reduce | flops 8 | bytes 64 | tf_op jit(solution)/shard_map/psum | solution.py:158
  468.3 40.5 %psum.62 = f32[8]{0:T(128)S(1)} all-reduce(f32[8]{0:T(128)S(1)} %broadcast_multiply_fusion.1), channel_id=1, replica_groups=mesh['row'=4,'col'=8] {'row','col'}, use_global_device_ids=true, to_apply=%region_37.38 | all-reduce | flops 8 | bytes 64 | tf_op jit(solution)/shard_map/psum | solution.py:147
  510.4 4.2 collective-permute-start.38
  516.0 4.1 collective-permute-done.39
  520.3 37.9 %psum.63 = f32[8]{0:T(128)S(1)} all-reduce(f32[8]{0:T(128)S(1)} %broadcast_multiply_fusion), channel_id=1, replica_groups=mesh['row'=4,'col'=8] {'row','col'}, use_global_device_ids=true, to_apply=%region_39.40 | all-reduce | flops 8 | bytes 64 | tf_op jit(solution)/shard_map/psum | solution.py:158
  (298 shorter events, 136.6 us)
Async XLA Ops:
  1.6 7.2 %collective-permute-start = (f32[2,1,128]{2,1,0:T(1,128)S(1)}, f32[2,1,128]{2,1,0:T(1,128)S(1)}, u32[]{:S(2)}, u32[]{:S(2)}) collective-permute-start(f32[2,1,128]{2,1,0:T(1,128)S(1)} %get-tuple-element.60), channel_id=1, source_target_pairs={{0,8},{8,16},{16,24},{1,9},{9,17},{17,25},{2,10},{10,18},{18,26},{... | collective-permute-start | bytes 3080 | tf_op jit(solution)/shard_map/ppermute | solution.py:17
  13.1 18.8 %collective-permute-start.2 = (f32[2,194,1]{2,1,0:T(8,128)S(1)}, f32[2,194,1]{2,1,0:T(8,128)S(1)}, u32[]{:S(2)}, u32[]{:S(2)}) collective-permute-start(f32[2,194,1]{2,1,0:T(8,128)S(1)} %get-tuple-element.58), channel_id=1, source_target_pairs={{0,1},{1,2},{2,3},{3,4},{4,5},{5,6},{6,7},{8,9},{9,10},{10,11},{11... | collective-permute-start | bytes 4664 | tf_op jit(solution)/shard_map/ppermute | solution.py:17
  14.4 17.5 %collective-permute-start.3 = (f32[2,194,1]{2,1,0:T(8,128)S(1)}, f32[2,194,1]{2,1,0:T(8,128)}, u32[]{:S(2)}, u32[]{:S(2)}) collective-permute-start(f32[2,194,1]{2,1,0:T(8,128)S(1)} %get-tuple-element.59), channel_id=1, source_target_pairs={{1,0},{2,1},{3,2},{4,3},{5,4},{6,5},{7,6},{9,8},{10,9},{11,10},{12... | collective-permute-start | bytes 4664 | tf_op jit(solution)/shard_map/ppermute | solution.py:20
  86.7 13.9 %collective-permute-start.4 = (f32[8,1,128]{1,0,2:T(8,128)S(1)}, f32[8,1,128]{1,0,2:T(8,128)S(1)}, u32[]{:S(2)}, u32[]{:S(2)}) collective-permute-start(f32[8,1,128]{1,0,2:T(8,128)S(1)} %get-tuple-element.25), channel_id=1, source_target_pairs={{0,8},{8,16},{16,24},{1,9},{9,17},{17,25},{2,10},{10,18},{18,26},{... | collective-permute-start | bytes 12296 | tf_op jit(solution)/shard_map/ppermute | solution.py:17
  90.2 15.1 %collective-permute-start.5 = (f32[8,1,128]{1,0,2:T(8,128)S(1)}, f32[8,1,128]{1,0,2:T(8,128)S(1)}, u32[]{:S(2)}, u32[]{:S(2)}) collective-permute-start(f32[8,1,128]{1,0,2:T(8,128)S(1)} %get-tuple-element.26), channel_id=1, source_target_pairs={{8,0},{16,8},{24,16},{9,1},{17,9},{25,17},{10,2},{18,10},{26,18},{... | collective-permute-start | bytes 12296 | tf_op jit(solution)/shard_map/ppermute | solution.py:20
  106.1 8.8 %collective-permute-start.6 = (f32[8,194,1]{1,0,2:T(8,128)S(1)}, f32[8,194,1]{1,0,2:T(8,128)S(1)}, u32[]{:S(2)}, u32[]{:S(2)}) collective-permute-start(f32[8,194,1]{1,0,2:T(8,128)S(1)} %get-tuple-element.23), channel_id=1, source_target_pairs={{0,1},{1,2},{2,3},{3,4},{4,5},{5,6},{6,7},{8,9},{9,10},{10,11},{11... | collective-permute-start | bytes 18632 | tf_op jit(solution)/shard_map/ppermute | solution.py:17
  109.4 6.0 %collective-permute-start.7 = (f32[8,194,1]{1,0,2:T(8,128)S(1)}, f32[8,194,1]{1,0,2:T(8,128)S(1)}, u32[]{:S(2)}, u32[]{:S(2)}) collective-permute-start(f32[8,194,1]{1,0,2:T(8,128)S(1)} %get-tuple-element.24), channel_id=1, source_target_pairs={{1,0},{2,1},{3,2},{4,3},{5,4},{6,5},{7,6},{9,8},{10,9},{11,10},{12... | collective-permute-start | bytes 18632 | tf_op jit(solution)/shard_map/ppermute | solution.py:20
  143.4 7.5 %collective-permute-start.8 = (f32[8,1,64]{1,2,0:T(8,128)S(1)}, f32[8,1,64]{1,2,0:T(8,128)S(1)}, u32[]{:S(2)}, u32[]{:S(2)}) collective-permute-start(f32[8,1,64]{1,2,0:T(8,128)S(1)} %get-tuple-element.33), channel_id=1, source_target_pairs={{0,8},{8,16},{16,24},{1,9},{9,17},{17,25},{2,10},{10,18},{18,26},{... | collective-permute-start | bytes 6152 | tf_op jit(solution)/shard_map/ppermute | solution.py:17
  146.9 8.7 %collective-permute-start.9 = (f32[8,1,64]{1,2,0:T(8,128)S(1)}, f32[8,1,64]{1,2,0:T(8,128)S(1)}, u32[]{:S(2)}, u32[]{:S(2)}) collective-permute-start(f32[8,1,64]{1,2,0:T(8,128)S(1)} %get-tuple-element.34), channel_id=1, source_target_pairs={{8,0},{16,8},{24,16},{9,1},{17,9},{25,17},{10,2},{18,10},{26,18},{... | collective-permute-start | bytes 6152 | tf_op jit(solution)/shard_map/ppermute | solution.py:20
  155.7 7.1 %collective-permute-start.10 = (f32[8,98,1]{1,2,0:T(1,128)S(1)}, f32[8,98,1]{1,2,0:T(1,128)S(1)}, u32[]{:S(2)}, u32[]{:S(2)}) collective-permute-start(f32[8,98,1]{1,2,0:T(1,128)S(1)} %get-tuple-element.27), channel_id=1, source_target_pairs={{0,1},{1,2},{2,3},{3,4},{4,5},{5,6},{6,7},{8,9},{9,10},{10,11},{11... | collective-permute-start | bytes 9416 | tf_op jit(solution)/shard_map/ppermute | solution.py:17
  159.8 6.7 %collective-permute-start.11 = (f32[8,98,1]{1,2,0:T(1,128)S(1)}, f32[8,98,1]{1,2,0:T(1,128)S(1)}, u32[]{:S(2)}, u32[]{:S(2)}) collective-permute-start(f32[8,98,1]{1,2,0:T(1,128)S(1)} %get-tuple-element.28), channel_id=1, source_target_pairs={{1,0},{2,1},{3,2},{4,3},{5,4},{6,5},{7,6},{9,8},{10,9},{11,10},{12... | collective-permute-start | bytes 9416 | tf_op jit(solution)/shard_map/ppermute | solution.py:20
  180.1 7.1 %collective-permute-start.13 = (f32[8,1,32]{1,2,0:T(8,128)S(1)}, f32[8,1,32]{1,2,0:T(8,128)S(1)}, u32[]{:S(2)}, u32[]{:S(2)}) collective-permute-start(f32[8,1,32]{1,2,0:T(8,128)S(1)} %get-tuple-element.95), channel_id=1, source_target_pairs={{8,0},{16,8},{24,16},{9,1},{17,9},{25,17},{10,2},{18,10},{26,18},{... | collective-permute-start | bytes 3080 | tf_op jit(solution)/shard_map/ppermute | solution.py:20
  187.4 5.7 %collective-permute-start.14 = (f32[8,50,1]{1,2,0:T(1,128)S(1)}, f32[8,50,1]{1,2,0:T(1,128)S(1)}, u32[]{:S(2)}, u32[]{:S(2)}) collective-permute-start(f32[8,50,1]{1,2,0:T(1,128)S(1)} %get-tuple-element.31), channel_id=1, source_target_pairs={{0,1},{1,2},{2,3},{3,4},{4,5},{5,6},{6,7},{8,9},{9,10},{10,11},{11... | collective-permute-start | bytes 4808 | tf_op jit(solution)/shard_map/ppermute | solution.py:17
  197.7 6.4 %collective-permute-start.16 = (f32[13,24,16]{0,2,1:T(8,128)S(1)}, f32[13,24,16]{0,2,1:T(8,128)S(1)}, u32[]{:S(2)}, u32[]{:S(2)}) collective-permute-start(f32[13,24,16]{0,2,1:T(8,128)S(1)} %concatenate.161), channel_id=1, source_target_pairs={{0,8},{8,0},{16,24},{24,16},{1,9},{9,1},{17,25},{25,17},{2,10},{10... | collective-permute-start | bytes 59912 | tf_op jit(solution)/shard_map/ppermute | solution.py:32
  207.0 11.3 %collective-permute-start.18 = (f32[8,1,32]{1,2,0:T(8,128)S(1)}, f32[8,1,32]{1,2,0:T(8,128)S(1)}, u32[]{:S(2)}, u32[]{:S(2)}) collective-permute-start(f32[8,1,32]{1,2,0:T(8,128)S(1)} %get-tuple-element.93), channel_id=1, source_target_pairs={{0,16},{8,24},{1,17},{9,25},{2,18},{10,26},{3,19},{11,27},{4,20},{... | collective-permute-start | bytes 3080 | tf_op jit(solution)/shard_map/ppermute | solution.py:28
  208.4 11.0 %collective-permute-start.19 = (f32[8,1,32]{1,2,0:T(8,128)S(1)}, f32[8,1,32]{1,2,0:T(8,128)S(1)}, u32[]{:S(2)}, u32[]{:S(2)}) collective-permute-start(f32[8,1,32]{1,2,0:T(8,128)S(1)} %get-tuple-element.92), channel_id=1, source_target_pairs={{16,0},{24,8},{17,1},{25,9},{18,2},{26,10},{19,3},{27,11},{20,4},{... | collective-permute-start | bytes 3080 | tf_op jit(solution)/shard_map/ppermute | solution.py:28
  209.7 9.7 %collective-permute-start.20 = (f32[8,48,1]{1,2,0:T(1,128)S(1)}, f32[8,48,1]{1,2,0:T(1,128)S(1)}, u32[]{:S(2)}, u32[]{:S(2)}) collective-permute-start(f32[8,48,1]{1,2,0:T(1,128)S(1)} %get-tuple-element.89), channel_id=1, source_target_pairs={{0,2},{1,3},{2,4},{3,5},{4,6},{5,7},{8,10},{9,11},{10,12},{11,13},... | collective-permute-start | bytes 4616 | tf_op jit(solution)/shard_map/ppermute | solution.py:28
  214.2 5.5 collective-permute-start.21
  221.6 11.2 %collective-permute-start.22 = (f32[13,24,16]{0,2,1:T(8,128)S(1)}, f32[13,24,16]{0,2,1:T(8,128)S(1)}, u32[]{:S(2)}, u32[]{:S(2)}) collective-permute-start(f32[13,24,16]{0,2,1:T(8,128)S(1)} %concatenate.170), channel_id=1, source_target_pairs={{0,16},{8,24},{16,0},{24,8},{1,17},{9,25},{17,1},{25,9},{2,18},{10... | collective-permute-start | bytes 59912 | tf_op jit(solution)/shard_map/ppermute | solution.py:32
  238.8 6.0 %collective-permute-start.24 = (f32[8,1,32]{1,2,0:T(8,128)S(1)}, f32[8,1,32]{1,2,0:T(8,128)S(1)}, u32[]{:S(2)}, u32[]{:S(2)}) collective-permute-start(f32[8,1,32]{1,2,0:T(8,128)S(1)} %get-tuple-element.40), channel_id=1, source_target_pairs={} | collective-permute-start | bytes 3080 | tf_op jit(solution)/shard_map/ppermute | solution.py:28
  243.5 5.5 collective-permute-start.27
  327.9 6.8 %collective-permute-start.28 = (f32[8,1,32]{1,2,0:T(8,128)S(1)}, f32[8,1,32]{1,2,0:T(8,128)S(1)}, u32[]{:S(2)}, u32[]{:S(2)}) collective-permute-start(f32[8,1,32]{1,2,0:T(8,128)S(1)} %get-tuple-element.78), channel_id=1, source_target_pairs={} | collective-permute-start | bytes 3080 | tf_op jit(solution)/shard_map/ppermute | solution.py:28
  328.5 6.2 %collective-permute-start.29 = (f32[8,1,32]{1,2,0:T(8,128)S(1)}, f32[8,1,32]{1,2,0:T(8,128)S(1)}, u32[]{:S(2)}, u32[]{:S(2)}) collective-permute-start(f32[8,1,32]{1,2,0:T(8,128)S(1)} %get-tuple-element.79), channel_id=1, source_target_pairs={} | collective-permute-start | bytes 3080 | tf_op jit(solution)/shard_map/ppermute | solution.py:28
  329.2 5.5 collective-permute-start.30
  333.4 5.5 collective-permute-start.31
  419.2 6.8 %collective-permute-start.32 = (f32[8,1,32]{1,2,0:T(8,128)S(1)}, f32[8,1,32]{1,2,0:T(8,128)S(1)}, u32[]{:S(2)}, u32[]{:S(2)}) collective-permute-start(f32[8,1,32]{1,2,0:T(8,128)S(1)} %get-tuple-element.70), channel_id=1, source_target_pairs={} | collective-permute-start | bytes 3080 | tf_op jit(solution)/shard_map/ppermute | solution.py:28
  419.9 6.2 %collective-permute-start.33 = (f32[8,1,32]{1,2,0:T(8,128)S(1)}, f32[8,1,32]{1,2,0:T(8,128)S(1)}, u32[]{:S(2)}, u32[]{:S(2)}) collective-permute-start(f32[8,1,32]{1,2,0:T(8,128)S(1)} %get-tuple-element.71), channel_id=1, source_target_pairs={} | collective-permute-start | bytes 3080 | tf_op jit(solution)/shard_map/ppermute | solution.py:28
  420.5 5.5 collective-permute-start.34
  509.1 6.9 %collective-permute-start.36 = (f32[8,1,32]{1,2,0:T(8,128)S(1)}, f32[8,1,32]{1,2,0:T(8,128)S(1)}, u32[]{:S(2)}, u32[]{:S(2)}) collective-permute-start(f32[8,1,32]{1,2,0:T(8,128)S(1)} %get-tuple-element.69), channel_id=1, source_target_pairs={} | collective-permute-start | bytes 3080 | tf_op jit(solution)/shard_map/ppermute | solution.py:28
  509.7 6.3 %collective-permute-start.37 = (f32[8,1,32]{1,2,0:T(8,128)S(1)}, f32[8,1,32]{1,2,0:T(8,128)S(1)}, u32[]{:S(2)}, u32[]{:S(2)}) collective-permute-start(f32[8,1,32]{1,2,0:T(8,128)S(1)} %get-tuple-element.68), channel_id=1, source_target_pairs={} | collective-permute-start | bytes 3080 | tf_op jit(solution)/shard_map/ppermute | solution.py:28
  510.4 5.6 collective-permute-start.38
  514.6 5.5 collective-permute-start.39
  (41 other events, 672.4 us)
where the time goes:
time: 573 us; the launch traced here: 563 us
  blocking collectives  274 us (48%)
  starting transfers between devices  78.8 us (14%)
  local copies, waits for them, and re-layouts  78.5 us (14%)
  waiting for transfers between devices  67.8 us (12%)
  other arithmetic  62.1 us (11%)
    psum x4, blocking collectives, norm_sum(): return lax.psum(local_dot(values, values), ('row', 'col'))  160 us
    psum x3, blocking collectives, coarse_solve(): step_size = norm_now / lax.psum(local_dot(direction, image), ('row', 'col'))  113 us
    ppermute x20, starting transfers between devices, shifted(): return lax.ppermute(block, axis, route)  35.1 us
    ppermute x8, starting transfers between devices, padded_2(): lax.ppermute(lax.slice_in_dim(block, block.shape[dim] - width, None, axis...  25.6 us
    ppermute x8, waiting for transfers between devices, padded_2(): lax.ppermute(lax.slice_in_dim(block, 0, width, axis=dim), axis, backward)  23 us
    reduce_sum x4, other arithmetic, restrict_field(): values.reshape(count, rows_here // 2, 2, cols_here // 2, 2).sum(axis=(2, 4))  19.1 us
    ppermute x20, waiting for transfers between devices, shifted(): return lax.ppermute(block, axis, route)  17.9 us
    ppermute x4, waiting for transfers between devices, partner_2(): lax.ppermute(shard, axis, [(i, i ^ 1 << apart) for i in range(lax.axis_si...  17.4 us
  transfers between devices with their start and end apart: 40, of which 19 were waited for; matrix products, arithmetic and copies ran while one was open for 6% of the time, Pallas kernels for 0%

commit v1 on v0

--- a/solution.py
+++ b/solution.py
@@ -155,7 +155,7 @@
     norm_now = norm_sum(residual)
     for sweep in range(ITERS):
         image = apply_operator(direction, coeffs, sides_of(direction))
-        step_size = norm_now / lax.psum(local_dot(direction, image), ("row", "col"))
+        step_size = norm_now / lax.psum(lax.psum(local_dot(direction, image), "col"), "row")
         solution = solution + expand(step_size) * direction
         if sweep + 1 < ITERS:
             residual = residual - expand(step_size) * image

time: 573 us -> 541 us (0.944)
  blocking collectives: 274 us -> 242 us
    psum x3 -> x8, blocking collectives: 113 us -> 88.2 us  [the longest x4 47.2 us: coarse_solve(): lax.psum(local_dot(direction, image), 'col')]
    psum x4, blocking collectives: 160 us -> 154 us  [norm_sum(): return lax.psum(local_dot(values, values), ('row', 'col'))]
where the time goes in v1:
time: 541 us; the launch traced here: 531 us
  blocking collectives  242 us (45%)
  local copies, waits for them, and re-layouts  78.9 us (15%)
  starting transfers between devices  78.7 us (15%)
  waiting for transfers between devices  67.9 us (13%)
  other arithmetic  62.1 us (11%)
    psum x4, blocking collectives, norm_sum(): return lax.psum(local_dot(values, values), ('row', 'col'))  154 us
    psum x4, blocking collectives, coarse_solve(): lax.psum(local_dot(direction, image), 'col')  47.2 us
    psum x4, blocking collectives, coarse_solve(): lax.psum(lax.psum(local_dot(direction, image), 'col'), 'row')  41.1 us
    ppermute x20, starting transfers between devices, shifted(): return lax.ppermute(block, axis, route)  35 us
    ppermute x8, starting transfers between devices, padded_2(): lax.ppermute(lax.slice_in_dim(block, block.shape[dim] - width, None, axis...  25.6 us
    ppermute x8, waiting for transfers between devices, padded_2(): lax.ppermute(lax.slice_in_dim(block, 0, width, axis=dim), axis, backward)  23 us
    reduce_sum x4, other arithmetic, restrict_field(): values.reshape(count, rows_here // 2, 2, cols_here // 2, 2).sum(axis=(2, 4))  19.1 us
    ppermute x20, waiting for transfers between devices, shifted(): return lax.ppermute(block, axis, route)  17.9 us
  transfers between devices with their start and end apart: 40, of which 19 were waited for; matrix products, arithmetic and copies ran while one was open for 6% of the time, Pallas kernels for 0%

profile of v1, /device:TPU:0, one launch (start us, length us, event | category | flops | bytes accessed | tf_op | source)
XLA Modules:
  0.0 531.5 jit_solution(14172915156742882052)
XLA Ops:
  1.6 4.9 collective-permute-start
  17.3 8.4 %squeeze.46 = f32[96,2,64,2]{3,2,1,0:T(8,128)} reshape(f32[192,128]{1,0:T(8,128)} %param.5) | data formatting | bytes 196608 | tf_op jit(solution)/shard_map/squeeze | solution.py:72
  34.1 7.6 %squeeze.47 = f32[96,2,64,2]{3,2,1,0:T(8,128)} reshape(f32[192,128]{1,0:T(8,128)S(1)} %get-tuple-element.17) | data formatting | bytes 196608 | tf_op jit(solution)/shard_map/squeeze | solution.py:73
  41.6 7.6 %squeeze.48 = f32[96,2,64,2]{3,2,1,0:T(8,128)} reshape(f32[192,128]{1,0:T(8,128)S(1)} %get-tuple-element.18) | data formatting | bytes 196608 | tf_op jit(solution)/shard_map/squeeze | solution.py:74
  49.2 4.6 slice_reduce_fusion.2
  54.0 7.6 %squeeze.49 = f32[96,2,64,2]{3,2,1,0:T(8,128)} reshape(f32[192,128]{1,0:T(8,128)S(1)} %get-tuple-element.19) | data formatting | bytes 196608 | tf_op jit(solution)/shard_map/squeeze | solution.py:75
  61.6 8.1 %squeeze.50 = f32[96,2,64,2]{3,2,1,0:T(8,128)} reshape(f32[192,128]{1,0:T(8,128)S(1)} %get-tuple-element.20) | data formatting | bytes 196608 | tf_op jit(solution)/shard_map/squeeze | solution.py:76
  69.7 7.9 %slice_reduce_fusion = (f32[96,64]{1,0:T(8,128)S(1)}, f32[96,64]{1,0:T(8,128)S(1)}) fusion(f32[96,2,64,2]{3,2,1,0:T(8,128)} %squeeze.50, f32[96,2,64,2]{3,2,1,0:T(8,128)} %squeeze.49), kind=kLoop, calls=%fused_computation | loop fusion | flops 12288 | bytes 147456 | tf_op jit(solution)/shard_map/reduce_sum | solution.py:76
  92.2 8.8 %collective-permute-done.4 = f32[8,1,128]{1,0,2:T(8,128)S(1)} collective-permute-done((f32[8,1,128]{1,0,2:T(8,128)S(1)}, f32[8,1,128]{1,0,2:T(8,128)S(1)}, u32[]{:S(2)}, u32[]{:S(2)}) %collective-permute-start.4) | collective-permute-done | bytes 4128 | tf_op jit(solution)/shard_map/ppermute | solution.py:17
  101.0 4.7 collective-permute-done.5
  119.9 7.0 %copy.453 = f32[8,192,128]{0,2,1:T(8,128)} copy(f32[8,192,128]{1,0,2:T(8,128)S(1)} %fusion.3) | data formatting | bytes 1572864 | tf_op jit(solution)/shard_map/sub | solution.py:103
  126.9 14.0 %reduce_sum.288 = f32[8,96,64]{0,2,1:T(8,128)S(1)} reduce(f32[8,96,2,64,2]{0,4,3,2,1:T(2,128)} %bitcast.80, f32[]{:T(128)} %constant.67.clone.1), dimensions={2,4}, to_apply=%region_0.0 | reduce | flops 147456 | bytes 983044 | tf_op jit(solution)/shard_map/reduce_sum | solution.py:66
  151.3 4.7 collective-permute-done.9
  198.6 5.9 %collective-permute-done.16 = f32[13,24,16]{0,2,1:T(8,128)S(1)} collective-permute-done((f32[13,24,16]{0,2,1:T(8,128)S(1)}, f32[13,24,16]{0,2,1:T(8,128)S(1)}, u32[]{:S(2)}, u32[]{:S(2)}) %collective-permute-start.16) | collective-permute-done | bytes 20000 | tf_op jit(solution)/shard_map/ppermute | solution.py:32
  210.0 4.5 collective-permute-start.20
  225.7 7.4 %collective-permute-done.22 = f32[13,24,16]{0,2,1:T(8,128)S(1)} collective-permute-done((f32[13,24,16]{0,2,1:T(8,128)S(1)}, f32[13,24,16]{0,2,1:T(8,128)S(1)}, u32[]{:S(2)}, u32[]{:S(2)}) %collective-permute-start.22) | collective-permute-done | bytes 20000 | tf_op jit(solution)/shard_map/ppermute | solution.py:32
  245.2 4.2 collective-permute-done.27
  249.6 11.8 %psum.85 = f32[8]{0:T(128)S(1)} all-reduce(f32[8]{0:T(128)S(1)} %broadcast_multiply_fusion.6), channel_id=1, replica_groups=mesh['row'=4,'col'=8] {'col'}, use_global_device_ids=true, to_apply=%region_27.28 | all-reduce | flops 8 | bytes 64 | tf_op jit(solution)/shard_map/psum | solution.py:158
  261.4 10.8 %psum.86 = f32[8]{0:T(128)S(1)} all-reduce(f32[8]{0:T(128)S(1)} %psum.85), channel_id=1, replica_groups=mesh['row'=4,'col'=8] {'row'}, use_global_device_ids=true, to_apply=%region_28.29 | all-reduce | flops 8 | bytes 64 | tf_op jit(solution)/shard_map/psum | solution.py:158
  272.2 37.2 %psum.84 = f32[8]{0:T(128)S(1)} all-reduce(f32[8]{0:T(128)S(1)} %broadcast_multiply_fusion.7), channel_id=1, replica_groups=mesh['row'=4,'col'=8] {'row','col'}, use_global_device_ids=true, to_apply=%region_25.26 | all-reduce | flops 8 | bytes 64 | tf_op jit(solution)/shard_map/psum | solution.py:147
  309.6 40.6 %psum.87 = f32[8]{0:T(128)S(1)} all-reduce(f32[8]{0:T(128)S(1)} %broadcast_multiply_fusion.5), channel_id=1, replica_groups=mesh['row'=4,'col'=8] {'row','col'}, use_global_device_ids=true, to_apply=%region_30.31 | all-reduce | flops 8 | bytes 64 | tf_op jit(solution)/shard_map/psum | solution.py:147
  351.9 4.2 collective-permute-start.30
  361.8 11.8 %psum.88 = f32[8]{0:T(128)S(1)} all-reduce(f32[8]{0:T(128)S(1)} %broadcast_multiply_fusion.4), channel_id=1, replica_groups=mesh['row'=4,'col'=8] {'col'}, use_global_device_ids=true, to_apply=%region_32.33 | all-reduce | flops 8 | bytes 64 | tf_op jit(solution)/shard_map/psum | solution.py:158
  373.6 9.9 %psum.89 = f32[8]{0:T(128)S(1)} all-reduce(f32[8]{0:T(128)S(1)} %psum.88), channel_id=1, replica_groups=mesh['row'=4,'col'=8] {'row'}, use_global_device_ids=true, to_apply=%region_33.34 | all-reduce | flops 8 | bytes 64 | tf_op jit(solution)/shard_map/psum | solution.py:158
  383.8 38.1 %psum.90 = f32[8]{0:T(128)S(1)} all-reduce(f32[8]{0:T(128)S(1)} %broadcast_multiply_fusion.3), channel_id=1, replica_groups=mesh['row'=4,'col'=8] {'row','col'}, use_global_device_ids=true, to_apply=%region_35.36 | all-reduce | flops 8 | bytes 64 | tf_op jit(solution)/shard_map/psum | solution.py:147
  423.5 4.2 collective-permute-start.34
  433.4 11.8 %psum.91 = f32[8]{0:T(128)S(1)} all-reduce(f32[8]{0:T(128)S(1)} %broadcast_multiply_fusion.2), channel_id=1, replica_groups=mesh['row'=4,'col'=8] {'col'}, use_global_device_ids=true, to_apply=%region_37.38 | all-reduce | flops 8 | bytes 64 | tf_op jit(solution)/shard_map/psum | solution.py:158
  445.2 10.0 %psum.92 = f32[8]{0:T(128)S(1)} all-reduce(f32[8]{0:T(128)S(1)} %psum.91), channel_id=1, replica_groups=mesh['row'=4,'col'=8] {'row'}, use_global_device_ids=true, to_apply=%region_38.39 | all-reduce | flops 8 | bytes 64 | tf_op jit(solution)/shard_map/psum | solution.py:158
  455.5 38.0 %psum.93 = f32[8]{0:T(128)S(1)} all-reduce(f32[8]{0:T(128)S(1)} %broadcast_multiply_fusion.1), channel_id=1, replica_groups=mesh['row'=4,'col'=8] {'row','col'}, use_global_device_ids=true, to_apply=%region_40.41 | all-reduce | flops 8 | bytes 64 | tf_op jit(solution)/shard_map/psum | solution.py:147
  495.1 4.2 collective-permute-start.38
  505.0 11.8 %psum.94 = f32[8]{0:T(128)S(1)} all-reduce(f32[8]{0:T(128)S(1)} %broadcast_multiply_fusion), channel_id=1, replica_groups=mesh['row'=4,'col'=8] {'col'}, use_global_device_ids=true, to_apply=%region_42.43 | all-reduce | flops 8 | bytes 64 | tf_op jit(solution)/shard_map/psum | solution.py:158
  516.8 10.3 %psum.95 = f32[8]{0:T(128)S(1)} all-reduce(f32[8]{0:T(128)S(1)} %psum.94), channel_id=1, replica_groups=mesh['row'=4,'col'=8] {'row'}, use_global_device_ids=true, to_apply=%region_43.44 | all-reduce | flops 8 | bytes 64 | tf_op jit(solution)/shard_map/psum | solution.py:158
  (303 shorter events, 157.1 us)
Async XLA Ops:
  1.6 7.2 %collective-permute-start = (f32[2,1,128]{2,1,0:T(1,128)S(1)}, f32[2,1,128]{2,1,0:T(1,128)S(1)}, u32[]{:S(2)}, u32[]{:S(2)}) collective-permute-start(f32[2,1,128]{2,1,0:T(1,128)S(1)} %get-tuple-element.58), channel_id=1, source_target_pairs={{0,8},{8,16},{16,24},{1,9},{9,17},{17,25},{2,10},{10,18},{18,26},{... | collective-permute-start | bytes 3080 | tf_op jit(solution)/shard_map/ppermute | solution.py:17
  13.1 18.8 %collective-permute-start.2 = (f32[2,194,1]{2,1,0:T(8,128)S(1)}, f32[2,194,1]{2,1,0:T(8,128)S(1)}, u32[]{:S(2)}, u32[]{:S(2)}) collective-permute-start(f32[2,194,1]{2,1,0:T(8,128)S(1)} %get-tuple-element.56), channel_id=1, source_target_pairs={{0,1},{1,2},{2,3},{3,4},{4,5},{5,6},{6,7},{8,9},{9,10},{10,11},{11... | collective-permute-start | bytes 4664 | tf_op jit(solution)/shard_map/ppermute | solution.py:17
  14.4 17.5 %collective-permute-start.3 = (f32[2,194,1]{2,1,0:T(8,128)S(1)}, f32[2,194,1]{2,1,0:T(8,128)}, u32[]{:S(2)}, u32[]{:S(2)}) collective-permute-start(f32[2,194,1]{2,1,0:T(8,128)S(1)} %get-tuple-element.57), channel_id=1, source_target_pairs={{1,0},{2,1},{3,2},{4,3},{5,4},{6,5},{7,6},{9,8},{10,9},{11,10},{12... | collective-permute-start | bytes 4664 | tf_op jit(solution)/shard_map/ppermute | solution.py:20
  87.1 13.9 %collective-permute-start.4 = (f32[8,1,128]{1,0,2:T(8,128)S(1)}, f32[8,1,128]{1,0,2:T(8,128)S(1)}, u32[]{:S(2)}, u32[]{:S(2)}) collective-permute-start(f32[8,1,128]{1,0,2:T(8,128)S(1)} %get-tuple-element.23), channel_id=1, source_target_pairs={{0,8},{8,16},{16,24},{1,9},{9,17},{17,25},{2,10},{10,18},{18,26},{... | collective-permute-start | bytes 12296 | tf_op jit(solution)/shard_map/ppermute | solution.py:17
  90.6 15.1 %collective-permute-start.5 = (f32[8,1,128]{1,0,2:T(8,128)S(1)}, f32[8,1,128]{1,0,2:T(8,128)S(1)}, u32[]{:S(2)}, u32[]{:S(2)}) collective-permute-start(f32[8,1,128]{1,0,2:T(8,128)S(1)} %get-tuple-element.24), channel_id=1, source_target_pairs={{8,0},{16,8},{24,16},{9,1},{17,9},{25,17},{10,2},{18,10},{26,18},{... | collective-permute-start | bytes 12296 | tf_op jit(solution)/shard_map/ppermute | solution.py:20
  106.5 8.8 %collective-permute-start.6 = (f32[8,194,1]{1,0,2:T(8,128)S(1)}, f32[8,194,1]{1,0,2:T(8,128)S(1)}, u32[]{:S(2)}, u32[]{:S(2)}) collective-permute-start(f32[8,194,1]{1,0,2:T(8,128)S(1)} %get-tuple-element.21), channel_id=1, source_target_pairs={{0,1},{1,2},{2,3},{3,4},{4,5},{5,6},{6,7},{8,9},{9,10},{10,11},{11... | collective-permute-start | bytes 18632 | tf_op jit(solution)/shard_map/ppermute | solution.py:17
  109.8 6.0 %collective-permute-start.7 = (f32[8,194,1]{1,0,2:T(8,128)S(1)}, f32[8,194,1]{1,0,2:T(8,128)S(1)}, u32[]{:S(2)}, u32[]{:S(2)}) collective-permute-start(f32[8,194,1]{1,0,2:T(8,128)S(1)} %get-tuple-element.22), channel_id=1, source_target_pairs={{1,0},{2,1},{3,2},{4,3},{5,4},{6,5},{7,6},{9,8},{10,9},{11,10},{12... | collective-permute-start | bytes 18632 | tf_op jit(solution)/shard_map/ppermute | solution.py:20
  143.8 7.5 %collective-permute-start.8 = (f32[8,1,64]{1,2,0:T(8,128)S(1)}, f32[8,1,64]{1,2,0:T(8,128)S(1)}, u32[]{:S(2)}, u32[]{:S(2)}) collective-permute-start(f32[8,1,64]{1,2,0:T(8,128)S(1)} %get-tuple-element.31), channel_id=1, source_target_pairs={{0,8},{8,16},{16,24},{1,9},{9,17},{17,25},{2,10},{10,18},{18,26},{... | collective-permute-start | bytes 6152 | tf_op jit(solution)/shard_map/ppermute | solution.py:17
  147.2 8.7 %collective-permute-start.9 = (f32[8,1,64]{1,2,0:T(8,128)S(1)}, f32[8,1,64]{1,2,0:T(8,128)S(1)}, u32[]{:S(2)}, u32[]{:S(2)}) collective-permute-start(f32[8,1,64]{1,2,0:T(8,128)S(1)} %get-tuple-element.32), channel_id=1, source_target_pairs={{8,0},{16,8},{24,16},{9,1},{17,9},{25,17},{10,2},{18,10},{26,18},{... | collective-permute-start | bytes 6152 | tf_op jit(solution)/shard_map/ppermute | solution.py:20
  156.1 7.1 %collective-permute-start.10 = (f32[8,98,1]{1,2,0:T(1,128)S(1)}, f32[8,98,1]{1,2,0:T(1,128)S(1)}, u32[]{:S(2)}, u32[]{:S(2)}) collective-permute-start(f32[8,98,1]{1,2,0:T(1,128)S(1)} %get-tuple-element.25), channel_id=1, source_target_pairs={{0,1},{1,2},{2,3},{3,4},{4,5},{5,6},{6,7},{8,9},{9,10},{10,11},{11... | collective-permute-start | bytes 9416 | tf_op jit(solution)/shard_map/ppermute | solution.py:17
  160.2 6.7 %collective-permute-start.11 = (f32[8,98,1]{1,2,0:T(1,128)S(1)}, f32[8,98,1]{1,2,0:T(1,128)S(1)}, u32[]{:S(2)}, u32[]{:S(2)}) collective-permute-start(f32[8,98,1]{1,2,0:T(1,128)S(1)} %get-tuple-element.26), channel_id=1, source_target_pairs={{1,0},{2,1},{3,2},{4,3},{5,4},{6,5},{7,6},{9,8},{10,9},{11,10},{12... | collective-permute-start | bytes 9416 | tf_op jit(solution)/shard_map/ppermute | solution.py:20
  180.5 7.1 %collective-permute-start.13 = (f32[8,1,32]{1,2,0:T(8,128)S(1)}, f32[8,1,32]{1,2,0:T(8,128)S(1)}, u32[]{:S(2)}, u32[]{:S(2)}) collective-permute-start(f32[8,1,32]{1,2,0:T(8,128)S(1)} %get-tuple-element.93), channel_id=1, source_target_pairs={{8,0},{16,8},{24,16},{9,1},{17,9},{25,17},{10,2},{18,10},{26,18},{... | collective-permute-start | bytes 3080 | tf_op jit(solution)/shard_map/ppermute | solution.py:20
  187.7 5.7 %collective-permute-start.14 = (f32[8,50,1]{1,2,0:T(1,128)S(1)}, f32[8,50,1]{1,2,0:T(1,128)S(1)}, u32[]{:S(2)}, u32[]{:S(2)}) collective-permute-start(f32[8,50,1]{1,2,0:T(1,128)S(1)} %get-tuple-element.29), channel_id=1, source_target_pairs={{0,1},{1,2},{2,3},{3,4},{4,5},{5,6},{6,7},{8,9},{9,10},{10,11},{11... | collective-permute-start | bytes 4808 | tf_op jit(solution)/shard_map/ppermute | solution.py:17
  198.0 6.4 %collective-permute-start.16 = (f32[13,24,16]{0,2,1:T(8,128)S(1)}, f32[13,24,16]{0,2,1:T(8,128)S(1)}, u32[]{:S(2)}, u32[]{:S(2)}) collective-permute-start(f32[13,24,16]{0,2,1:T(8,128)S(1)} %concatenate.161), channel_id=1, source_target_pairs={{0,8},{8,0},{16,24},{24,16},{1,9},{9,1},{17,25},{25,17},{2,10},{10... | collective-permute-start | bytes 59912 | tf_op jit(solution)/shard_map/ppermute | solution.py:32
  207.4 11.3 %collective-permute-start.18 = (f32[8,1,32]{1,2,0:T(8,128)S(1)}, f32[8,1,32]{1,2,0:T(8,128)S(1)}, u32[]{:S(2)}, u32[]{:S(2)}) collective-permute-start(f32[8,1,32]{1,2,0:T(8,128)S(1)} %get-tuple-element.91), channel_id=1, source_target_pairs={{0,16},{8,24},{1,17},{9,25},{2,18},{10,26},{3,19},{11,27},{4,20},{... | collective-permute-start | bytes 3080 | tf_op jit(solution)/shard_map/ppermute | solution.py:28
  208.7 11.0 %collective-permute-start.19 = (f32[8,1,32]{1,2,0:T(8,128)S(1)}, f32[8,1,32]{1,2,0:T(8,128)S(1)}, u32[]{:S(2)}, u32[]{:S(2)}) collective-permute-start(f32[8,1,32]{1,2,0:T(8,128)S(1)} %get-tuple-element.90), channel_id=1, source_target_pairs={{16,0},{24,8},{17,1},{25,9},{18,2},{26,10},{19,3},{27,11},{20,4},{... | collective-permute-start | bytes 3080 | tf_op jit(solution)/shard_map/ppermute | solution.py:28
  210.0 9.7 %collective-permute-start.20 = (f32[8,48,1]{1,2,0:T(1,128)S(1)}, f32[8,48,1]{1,2,0:T(1,128)S(1)}, u32[]{:S(2)}, u32[]{:S(2)}) collective-permute-start(f32[8,48,1]{1,2,0:T(1,128)S(1)} %get-tuple-element.87), channel_id=1, source_target_pairs={{0,2},{1,3},{2,4},{3,5},{4,6},{5,7},{8,10},{9,11},{10,12},{11,13},... | collective-permute-start | bytes 4616 | tf_op jit(solution)/shard_map/ppermute | solution.py:28
  214.6 5.5 %collective-permute-start.21 = (f32[8,48,1]{1,2,0:T(1,128)S(1)}, f32[8,48,1]{1,2,0:T(1,128)S(1)}, u32[]{:S(2)}, u32[]{:S(2)}) collective-permute-start(f32[8,48,1]{1,2,0:T(1,128)S(1)} %get-tuple-element.86), channel_id=1, source_target_pairs={{2,0},{3,1},{4,2},{5,3},{6,4},{7,5},{10,8},{11,9},{12,10},{13,11},... | collective-permute-start | bytes 4616 | tf_op jit(solution)/shard_map/ppermute | solution.py:28
  221.9 11.2 %collective-permute-start.22 = (f32[13,24,16]{0,2,1:T(8,128)S(1)}, f32[13,24,16]{0,2,1:T(8,128)S(1)}, u32[]{:S(2)}, u32[]{:S(2)}) collective-permute-start(f32[13,24,16]{0,2,1:T(8,128)S(1)} %concatenate.170), channel_id=1, source_target_pairs={{0,16},{8,24},{16,0},{24,8},{1,17},{9,25},{17,1},{25,9},{2,18},{10... | collective-permute-start | bytes 59912 | tf_op jit(solution)/shard_map/ppermute | solution.py:32
  239.1 6.0 %collective-permute-start.24 = (f32[8,1,32]{1,2,0:T(8,128)S(1)}, f32[8,1,32]{1,2,0:T(8,128)S(1)}, u32[]{:S(2)}, u32[]{:S(2)}) collective-permute-start(f32[8,1,32]{1,2,0:T(8,128)S(1)} %get-tuple-element.38), channel_id=1, source_target_pairs={} | collective-permute-start | bytes 3080 | tf_op jit(solution)/shard_map/ppermute | solution.py:28
  243.8 5.5 %collective-permute-start.27 = (f32[8,48,1]{1,2,0:T(1,128)S(1)}, f32[8,48,1]{1,2,0:T(1,128)S(1)}, u32[]{:S(2)}, u32[]{:S(2)}) collective-permute-start(f32[8,48,1]{1,2,0:T(1,128)S(1)} %get-tuple-element.43), channel_id=1, source_target_pairs={{4,0},{5,1},{6,2},{7,3},{12,8},{13,9},{14,10},{15,11},{20,16},{21,... | collective-permute-start | bytes 4616 | tf_op jit(solution)/shard_map/ppermute | solution.py:28
  350.6 6.8 %collective-permute-start.28 = (f32[8,1,32]{1,2,0:T(8,128)S(1)}, f32[8,1,32]{1,2,0:T(8,128)S(1)}, u32[]{:S(2)}, u32[]{:S(2)}) collective-permute-start(f32[8,1,32]{1,2,0:T(8,128)S(1)} %get-tuple-element.76), channel_id=1, source_target_pairs={} | collective-permute-start | bytes 3080 | tf_op jit(solution)/shard_map/ppermute | solution.py:28
  351.2 6.2 %collective-permute-start.29 = (f32[8,1,32]{1,2,0:T(8,128)S(1)}, f32[8,1,32]{1,2,0:T(8,128)S(1)}, u32[]{:S(2)}, u32[]{:S(2)}) collective-permute-start(f32[8,1,32]{1,2,0:T(8,128)S(1)} %get-tuple-element.77), channel_id=1, source_target_pairs={} | collective-permute-start | bytes 3080 | tf_op jit(solution)/shard_map/ppermute | solution.py:28
  351.9 5.5 %collective-permute-start.30 = (f32[8,48,1]{1,2,0:T(1,128)S(1)}, f32[8,48,1]{1,2,0:T(1,128)S(1)}, u32[]{:S(2)}, u32[]{:S(2)}) collective-permute-start(f32[8,48,1]{1,2,0:T(1,128)S(1)} %get-tuple-element.80), channel_id=1, source_target_pairs={{0,4},{1,5},{2,6},{3,7},{8,12},{9,13},{10,14},{11,15},{16,20},{17,... | collective-permute-start | bytes 4616 | tf_op jit(solution)/shard_map/ppermute | solution.py:28
  356.1 5.5 %collective-permute-start.31 = (f32[8,48,1]{1,2,0:T(1,128)S(1)}, f32[8,48,1]{1,2,0:T(1,128)S(1)}, u32[]{:S(2)}, u32[]{:S(2)}) collective-permute-start(f32[8,48,1]{1,2,0:T(1,128)S(1)} %get-tuple-element.81), channel_id=1, source_target_pairs={{4,0},{5,1},{6,2},{7,3},{12,8},{13,9},{14,10},{15,11},{20,16},{21,... | collective-permute-start | bytes 4616 | tf_op jit(solution)/shard_map/ppermute | solution.py:28
  422.2 6.8 %collective-permute-start.32 = (f32[8,1,32]{1,2,0:T(8,128)S(1)}, f32[8,1,32]{1,2,0:T(8,128)S(1)}, u32[]{:S(2)}, u32[]{:S(2)}) collective-permute-start(f32[8,1,32]{1,2,0:T(8,128)S(1)} %get-tuple-element.68), channel_id=1, source_target_pairs={} | collective-permute-start | bytes 3080 | tf_op jit(solution)/shard_map/ppermute | solution.py:28
  422.8 6.2 %collective-permute-start.33 = (f32[8,1,32]{1,2,0:T(8,128)S(1)}, f32[8,1,32]{1,2,0:T(8,128)S(1)}, u32[]{:S(2)}, u32[]{:S(2)}) collective-permute-start(f32[8,1,32]{1,2,0:T(8,128)S(1)} %get-tuple-element.69), channel_id=1, source_target_pairs={} | collective-permute-start | bytes 3080 | tf_op jit(solution)/shard_map/ppermute | solution.py:28
  423.5 5.5 %collective-permute-start.34 = (f32[8,48,1]{1,2,0:T(1,128)S(1)}, f32[8,48,1]{1,2,0:T(1,128)S(1)}, u32[]{:S(2)}, u32[]{:S(2)}) collective-permute-start(f32[8,48,1]{1,2,0:T(1,128)S(1)} %get-tuple-element.72), channel_id=1, source_target_pairs={{0,4},{1,5},{2,6},{3,7},{8,12},{9,13},{10,14},{11,15},{16,20},{17,... | collective-permute-start | bytes 4616 | tf_op jit(solution)/shard_map/ppermute | solution.py:28
  493.7 6.9 %collective-permute-start.36 = (f32[8,1,32]{1,2,0:T(8,128)S(1)}, f32[8,1,32]{1,2,0:T(8,128)S(1)}, u32[]{:S(2)}, u32[]{:S(2)}) collective-permute-start(f32[8,1,32]{1,2,0:T(8,128)S(1)} %get-tuple-element.67), channel_id=1, source_target_pairs={} | collective-permute-start | bytes 3080 | tf_op jit(solution)/shard_map/ppermute | solution.py:28
  494.4 6.3 %collective-permute-start.37 = (f32[8,1,32]{1,2,0:T(8,128)S(1)}, f32[8,1,32]{1,2,0:T(8,128)S(1)}, u32[]{:S(2)}, u32[]{:S(2)}) collective-permute-start(f32[8,1,32]{1,2,0:T(8,128)S(1)} %get-tuple-element.66), channel_id=1, source_target_pairs={} | collective-permute-start | bytes 3080 | tf_op jit(solution)/shard_map/ppermute | solution.py:28
  495.1 5.6 %collective-permute-start.38 = (f32[8,48,1]{1,2,0:T(1,128)S(1)}, f32[8,48,1]{1,2,0:T(1,128)S(1)}, u32[]{:S(2)}, u32[]{:S(2)}) collective-permute-start(f32[8,48,1]{1,2,0:T(1,128)S(1)} %get-tuple-element.63), channel_id=1, source_target_pairs={{0,4},{1,5},{2,6},{3,7},{8,12},{9,13},{10,14},{11,15},{16,20},{17,... | collective-permute-start | bytes 4616 | tf_op jit(solution)/shard_map/ppermute | solution.py:28
  499.2 5.5 %collective-permute-start.39 = (f32[8,48,1]{1,2,0:T(1,128)S(1)}, f32[8,48,1]{1,2,0:T(1,128)S(1)}, u32[]{:S(2)}, u32[]{:S(2)}) collective-permute-start(f32[8,48,1]{1,2,0:T(1,128)S(1)} %get-tuple-element.62), channel_id=1, source_target_pairs={{4,0},{5,1},{6,2},{7,3},{12,8},{13,9},{14,10},{15,11},{20,16},{21,... | collective-permute-start | bytes 4616 | tf_op jit(solution)/shard_map/ppermute | solution.py:28
  (41 other events, 673.7 us)
